TPU v7x, 256 devices: a whole 4x4x8 slice. The times are simulated.
256 devices in a mesh: frame: 16 (over z_hi, y, core), row: 16 (over x, z_lo).
Axes of the slice: x: 4, y: 4, z: 8 (z_hi: 2, z_lo: 4; z = z_hi * 4 + z_lo), core: 2. Of those that a mesh axis runs over, the one named last changes fastest.
Arguments:
- latent: bfloat16 [64, 32, 240, 320], P('frame', 'row'), may hold values from -6 to 6
- gain_one: float32 [320], replicated, may hold values from 0.1 to 1.9
- spatial_weight: bfloat16 [3, 3, 320, 320], replicated, may hold values from -0.109375 to 0.109375
- gain_two: float32 [320], replicated, may hold values from 0.1 to 1.9
- temporal_weight: bfloat16 [3, 320, 320], replicated, may hold values from -0.1875 to 0.1875
- gain_three: float32 [320], replicated, may hold values from 0.1 to 1.9
- query_weight: bfloat16 [320, 320], replicated, as said below
- key_weight: bfloat16 [320, 320], replicated, may hold values from -0.3125 to 0.3125
- value_weight: bfloat16 [320, 320], replicated, may hold values from -0.3125 to 0.3125
- out_weight: bfloat16 [320, 320], replicated, may hold values from -0.3125 to 0.3125
Outputs:
- block_out: float32 [64, 32, 240, 320], P('frame', 'row')
Inputs may be any that keep to these rules, and one draw needn't show every extreme that they name: `query_weight`: a projection matrix.
All inputs are finite; a program needn't handle non-finite values.
Results may differ from a plain program's by a relative error of at most 0.012.
The roundings to bfloat16 on the way count: a program that leaves them out, or rounds other values in their place, can miss the bound.
Values may be sent and summed in bfloat16 or wider, within the bound.
A program may use at most 128 MiB of HBM per device.

v0:
```python
import jax
import jax.numpy as jnp
from jax import lax
from jax.sharding import PartitionSpec as P

HEAD_DIM = 64


def extended(cells, sides, width):
    for axis, dim in sides:
        count = lax.axis_size(axis)
        ends = count - 1
        head = lax.slice_in_dim(cells, 0, width, axis=dim)
        tail = lax.slice_in_dim(cells, cells.shape[dim] - width, cells.shape[dim], axis=dim)
        cells = jnp.concatenate(
            [
                lax.ppermute(tail, axis, [(i, (i + 1) % count) for i in range(ends)]),
                cells,
                lax.ppermute(head, axis, [((i + 1) % count, i) for i in range(ends)]),
            ],
            axis=dim,
        )
    return cells


def rms_norm(values, gain):
    mean_sq = jnp.mean(values * values, axis=-1, keepdims=True)
    return values * lax.rsqrt(mean_sq + 1e-06) * gain


def project(normed, weight):
    chans = normed.shape[-1]
    flat = jnp.dot(normed.reshape(-1, chans), weight, preferred_element_type=jnp.float32)
    return flat.astype(jnp.bfloat16).reshape(normed.shape[:-1] + (weight.shape[1],))


def attend_heads(queries, keys, values):
    frames, pixels, chans = queries.shape
    heads = chans // HEAD_DIM
    q_split = queries.reshape(frames, pixels, heads, HEAD_DIM)
    k_split = keys.reshape(frames, pixels, heads, HEAD_DIM)
    v_split = values.reshape(frames, pixels, heads, HEAD_DIM)
    scores = jnp.einsum(
        "fphd,gphd->phfg", q_split, k_split, preferred_element_type=jnp.float32
    ) / jnp.sqrt(jnp.float32(HEAD_DIM))
    peak = jnp.max(scores, axis=-1, keepdims=True)
    expo = jnp.exp(scores - peak)
    total = jnp.sum(expo, axis=-1)
    weight = expo.astype(jnp.bfloat16)
    summed = jnp.einsum("phfg,gphd->fphd", weight, v_split, preferred_element_type=jnp.float32)
    summed = summed / jnp.transpose(total, (2, 0, 1))[..., None]
    return summed.reshape(frames, pixels, chans).astype(jnp.bfloat16)


def temporal_mix(padded, temporal_weight, frames):
    chans = padded.shape[-1]
    pixels = padded.shape[1]
    total = jnp.zeros((frames * pixels, chans), jnp.float32)
    for tap in range(3):
        total = total + jnp.dot(
            padded[tap : tap + frames].reshape(-1, chans),
            temporal_weight[tap],
            preferred_element_type=jnp.float32,
        )
    return total.reshape(frames, pixels, chans)


def local(
    latent,
    gain_one,
    spatial_weight,
    gain_two,
    temporal_weight,
    gain_three,
    query_weight,
    key_weight,
    value_weight,
    out_weight,
):
    frames_here, rows_here, width, chans = latent.shape
    source = latent.astype(jnp.float32)
    act_one = jax.nn.silu(rms_norm(source, gain_one)).astype(jnp.bfloat16)
    rimmed = extended(act_one, (("row", 1),), 1)
    spatial = lax.conv_general_dilated(
        rimmed,
        spatial_weight,
        (1, 1),
        ((0, 0), (1, 1)),
        dimension_numbers=("NHWC", "HWIO", "NHWC"),
        preferred_element_type=jnp.float32,
    )
    hidden_one = source + spatial
    pixels = rows_here * width
    hidden_flat = hidden_one.reshape(frames_here, pixels, chans)
    act_two = jax.nn.silu(rms_norm(hidden_flat, gain_two)).astype(jnp.bfloat16)
    padded = extended(act_two, (("frame", 0),), 1)
    temporal = temporal_mix(padded, temporal_weight, frames_here)
    hidden_two = hidden_flat + temporal
    normed = rms_norm(hidden_two, gain_three).astype(jnp.bfloat16)
    groups = lax.axis_size("frame")
    per_group = pixels // groups

    def attend_triple(triple):
        shape_in = triple[0].shape
        flat_q = triple[0].reshape(shape_in[0], shape_in[2], chans)
        flat_k = triple[1].reshape(shape_in[0], shape_in[2], chans)
        flat_v = triple[2].reshape(shape_in[0], shape_in[2], chans)
        return attend_heads(flat_q, flat_k, flat_v).reshape(shape_in)

    triple = (
        project(normed, query_weight).reshape(frames_here, groups, per_group, chans),
        project(normed, key_weight).reshape(frames_here, groups, per_group, chans),
        project(normed, value_weight).reshape(frames_here, groups, per_group, chans),
    )
    attended = attend_triple(
        (
            lax.all_to_all(triple[0], "frame", split_axis=1, concat_axis=0, tiled=True),
            lax.all_to_all(triple[1], "frame", split_axis=1, concat_axis=0, tiled=True),
            lax.all_to_all(triple[2], "frame", split_axis=1, concat_axis=0, tiled=True),
        )
    )
    returned = lax.all_to_all(attended, "frame", split_axis=0, concat_axis=1, tiled=True)
    mixed = jnp.dot(returned.reshape(-1, chans), out_weight, preferred_element_type=jnp.float32)
    result = hidden_two.reshape(-1, chans) + mixed
    return result.reshape(frames_here, rows_here, width, chans)


def solution(mesh):
    return jax.shard_map(
        local,
        mesh=mesh,
        in_specs=(P("frame", "row", None, None), P(), P(), P(), P(), P(), P(), P(), P(), P()),
        out_specs=P("frame", "row", None, None),
        check_vma=False,
    )
```

profile of v0, /device:TPU:39, one launch (start us, length us, event | category | flops | bytes accessed | tf_op | source)
XLA Modules:
  0.0 389.2 jit_solution(17123246703365757660)
XLA Ops:
  0.0 2.7 copy.64
  13.0 3.5 collective-permute-start
  16.5 11.6 %collective-permute-done.1 = bf16[4,1,240,320]{2,3,1,0:T(8,128)(2,1)} collective-permute-done((bf16[4,1,240,320]{2,3,1,0:T(8,128)(2,1)}, bf16[4,1,240,320]{2,3,1,0:T(8,128)(2,1)}, u32[]{:S(2)}, u32[]{:S(2)}) %collective-permute-start.1) | collective-permute-done | bytes 614432 | tf_op jit(solution)/shard_map/ppermute | solution.py:19
  29.5 15.3 %collective-permute-done = bf16[4,1,240,320]{2,3,1,0:T(8,128)(2,1)} collective-permute-done((bf16[4,1,240,320]{2,3,1,0:T(8,128)(2,1)}, bf16[4,1,240,320]{2,3,1,0:T(8,128)(2,1)}, u32[]{:S(2)}, u32[]{:S(2)}) %collective-permute-start) | collective-permute-done | bytes 614432 | tf_op jit(solution)/shard_map/ppermute | solution.py:17
  49.2 2.9 pad
  52.1 5.8 %reshape.116 = bf16[4,4,8,31,320]{4,3,2,1,0:T(8,128)(2,1)} reshape(bf16[4,4,248,320]{3,2,1,0:T(8,128)(2,1)} %pad) | data formatting | bytes 5079040 | tf_op jit(solution)/shard_map/conv_general_dilated | solution.py:84
  61.6 6.6 %fusion.24 = f32[2,32,31,320]{3,1,2,0:T(8,128)S(1)} fusion(bf16[3,3,320,320]{3,2,1,0:T(8,128)(2,1)S(1)} %copy-done, bf16[4,4,8,33,320]{4,3,2,1,0:T(8,128)(2,1)S(1)} %fusion.4, pred[32,31]{0,1:T(8,128)(4,1)S(1)} %copy-done.16), kind=kOutput, calls=%fused_computation.43 | convolution fusion | flops 3657543680 | bytes 7087072 | tf_op jit(solution)/shard_map/conv_general_dilated | solution.py:84
  71.7 2.8 multiply_reduce_fusion.2
  74.5 3.3 copy.72
  77.8 3.4 copy.71
  83.1 4.9 %copy.75 = bf16[4,2,240,320]{2,1,0,3:T(2,128)(2,1)} copy(bf16[4,2,240,320]{3,2,0,1:T(8,128)(2,1)} %multiply_convert_fusion) | data formatting | bytes 2457600 | tf_op jit(solution)/shard_map/convert_element_type | solution.py:95
  88.0 5.3 %convert_element_type.48 = bf16[1920,320]{0,1:T(8,128)(2,1)} reshape(bf16[4,2,240,320]{2,1,0,3:T(2,128)(2,1)} %copy.75) | data formatting | bytes 2457600 | tf_op jit(solution)/shard_map/convert_element_type | solution.py:95
  93.3 4.8 %reshape.108 = f32[4,480,320]{1,2,0:T(8,128)} reshape(f32[4,2,240,320]{2,1,3,0:T(2,128)} %copy.72) | data formatting | bytes 4915200 | tf_op jit(solution)/shard_map/reshape | solution.py:94
  98.2 2.6 multiply_convert_fusion.1
  102.9 3.4 collective-permute-start.3
  106.3 3.1 collective-permute-start.2
  109.4 5.1 %reshape.107 = f32[1920,320]{0,1:T(8,128)} reshape(f32[4,2,240,320]{2,1,0,3:T(2,128)} %copy.71) | data formatting | bytes 4915200 | tf_op jit(solution)/shard_map/reshape | solution.py:94
  114.5 3.7 fusion.32
  122.6 3.9 %reshape.109 = bf16[1920,320]{0,1:T(8,128)(2,1)} reshape(bf16[4,480,320]{1,0,2:T(4,128)(2,1)} %copy.74) | data formatting | bytes 2457600 | tf_op jit(solution)/shard_map/reshape | solution.py:61
  126.6 3.4 copy.76
  130.0 4.0 %reshape.110 = bf16[1920,320]{0,1:T(8,128)(2,1)} reshape(bf16[4,480,320]{1,0,2:T(4,128)(2,1)} %copy.76) | data formatting | bytes 2457600 | tf_op jit(solution)/shard_map/reshape | solution.py:61
  134.0 3.2 convolution_add_fusion.2
  137.2 3.3 convolution_add_fusion.1
  140.4 6.7 %reshape.111 = f32[4,2,240,320]{2,1,0,3:T(2,128)} reshape(f32[1920,320]{0,1:T(8,128)} %convolution_add_fusion.1) | data formatting | bytes 4915200 | tf_op jit(solution)/shard_map/reshape | solution.py:65
  147.1 5.7 %copy.77 = f32[4,2,240,320]{3,2,0,1:T(8,128)} copy(f32[4,2,240,320]{2,1,0,3:T(2,128)} %reshape.111) | data formatting | bytes 4915200 | tf_op jit(solution)/shard_map/reshape | solution.py:65
  155.3 4.3 %multiply_convert_fusion.2 = (bf16[1920,320]{0,1:T(8,128)(2,1)S(1)}, f32[1920,320]{0,1:T(8,128)}) fusion(f32[320]{0:T(512)S(1)} %copy-done.15, f32[1920]{0:T(1024)S(1)} %rsqrt.35, f32[1920,320]{0,1:T(8,128)} %reshape.107, f32[1920,320]{0,1:T(8,128)} %convolution_add_fusion.1), kind=kLoop, calls=%fused_computation.42 | loop fusion | flops 2457600 | bytes 8610560 | tf_op jit(solution)/shard_map/convert_element_type | solution.py:99
  162.0 2.5 reshape_reshape.22
  166.8 14.6 %all-to-all-start.2 = ((bf16[4,16,30,320]{3,0,2,1:T(4,128)(2,1)}), bf16[4,16,30,320]{3,0,2,1:T(4,128)(2,1)}, u32[]{:S(2)}, u32[]{:S(2)}) async-start(bf16[4,16,30,320]{3,0,2,1:T(4,128)(2,1)} %copy.86), calls=%async_computation.2 | async-start | bytes 2949120 | tf_op jit(solution)/shard_map/all_to_all | solution.py:118
  183.9 2.5 reshape_reshape.20
  188.7 32.6 %all-to-all-done.2 = bf16[4,16,30,320]{3,0,2,1:T(4,128)(2,1)} async-done(((bf16[4,16,30,320]{3,0,2,1:T(4,128)(2,1)}), bf16[4,16,30,320]{3,0,2,1:T(4,128)(2,1)}, u32[]{:S(2)}, u32[]{:S(2)}) %all-to-all-start.2) | async-done | bytes 1228832 | tf_op jit(solution)/shard_map/all_to_all | solution.py:118
  221.3 5.0 %all-to-all-start.1 = ((bf16[4,16,30,320]{3,0,2,1:T(4,128)(2,1)}), bf16[4,16,30,320]{3,0,2,1:T(4,128)(2,1)S(1)}, u32[]{:S(2)}, u32[]{:S(2)}) async-start(bf16[4,16,30,320]{3,0,2,1:T(4,128)(2,1)} %copy.83), calls=%async_computation.1 | async-start | bytes 2949120 | tf_op jit(solution)/shard_map/all_to_all | solution.py:117
  228.3 2.5 copy.79
  230.8 2.5 reshape_reshape.18
  235.7 27.8 %all-to-all-done.1 = bf16[4,16,30,320]{3,0,2,1:T(4,128)(2,1)S(1)} async-done(((bf16[4,16,30,320]{3,0,2,1:T(4,128)(2,1)}), bf16[4,16,30,320]{3,0,2,1:T(4,128)(2,1)S(1)}, u32[]{:S(2)}, u32[]{:S(2)}) %all-to-all-start.1) | async-done | bytes 1228832 | tf_op jit(solution)/shard_map/all_to_all | solution.py:117
  263.5 5.3 %all-to-all-start = ((bf16[4,16,30,320]{3,0,2,1:T(4,128)(2,1)}), bf16[4,16,30,320]{3,0,2,1:T(4,128)(2,1)S(1)}, u32[]{:S(2)}, u32[]{:S(2)}) async-start(bf16[4,16,30,320]{3,0,2,1:T(4,128)(2,1)} %copy.80), calls=%async_computation | async-start | bytes 2949120 | tf_op jit(solution)/shard_map/all_to_all | solution.py:119
  268.8 3.3 copy.87
  272.1 5.5 %reshape_reshape.23 = bf16[64,30,5,64]{3,2,0,1:T(8,128)(2,1)} reshape(bf16[16,4,1,30,320]{4,1,0,3,2:T(4,128)(2,1)} %copy.87) | data formatting | bytes 2457600 | tf_op jit(solution)/shard_map/reshape;reshape | solution.py:41
  279.6 5.5 %reshape_reshape.21 = bf16[64,30,5,64]{3,2,0,1:T(8,128)(2,1)} reshape(bf16[16,4,1,30,320]{4,1,0,3,2:T(4,128)(2,1)} %copy.84) | data formatting | bytes 2457600 | tf_op jit(solution)/shard_map/reshape;reshape | solution.py:40
  285.1 20.7 %all-to-all-done = bf16[4,16,30,320]{3,0,2,1:T(4,128)(2,1)S(1)} async-done(((bf16[4,16,30,320]{3,0,2,1:T(4,128)(2,1)}), bf16[4,16,30,320]{3,0,2,1:T(4,128)(2,1)S(1)}, u32[]{:S(2)}, u32[]{:S(2)}) %all-to-all-start) | async-done | bytes 1228832 | tf_op jit(solution)/shard_map/all_to_all | solution.py:119
  306.6 3.6 reshape_reshape.19
  310.2 4.7 %multiply_reduce_fusion = (f32[30,5,64]{2,1,0:T(8,128)S(1)}, f32[30,5,64,64]{2,3,1,0:T(8,128)S(1)}) fusion(bf16[64,30,5,64]{3,2,0,1:T(8,128)(2,1)} %reshape_reshape.23, bf16[64,30,5,64]{3,2,0,1:T(8,128)(2,1)} %reshape_reshape.21), kind=kOutput, calls=%fused_computation.5 | convolution fusion | flops 79862400 | bytes 4953600 | tf_op jit(solution)/shard_map/fphd,gphd->phfg/dot_general | solution.py:43
  317.1 2.7 fusion.1
  319.8 3.9 %copy.92 = bf16[64,1,30,320]{3,2,1,0:T(8,128)(2,1)S(1)} copy(bf16[64,1,30,320]{0,3,2,1:T(8,128)(2,1)} %bitcast.80) | data formatting | bytes 2457600 | tf_op jit(solution)/shard_map/convert_element_type | solution.py:52
  323.7 44.2 %all_to_all.60 = bf16[64,1,30,320]{3,2,1,0:T(8,128)(2,1)S(1)} all-to-all(bf16[64,1,30,320]{3,2,1,0:T(8,128)(2,1)S(1)} %copy.92), channel_id=1, replica_groups=mesh['frame'=16,'row'=16] {'frame'}, dimensions={0} | all-to-all | bytes 2457600 | tf_op jit(solution)/shard_map/all_to_all | solution.py:122
  370.7 3.5 reshape.112
  374.3 3.7 convolution_add_fusion
  378.0 6.9 %reshape.113 = f32[4,2,240,320]{2,1,0,3:T(2,128)} reshape(f32[1920,320]{0,1:T(8,128)} %convolution_add_fusion) | data formatting | bytes 4915200 | tf_op jit(solution)/shard_map/reshape | solution.py:125
  384.9 4.1 %copy.95 = f32[4,2,240,320]{2,3,1,0:T(8,128)} copy(f32[4,2,240,320]{2,1,0,3:T(2,128)} %reshape.113) | data formatting | bytes 4915200 | tf_op jit(solution)/shard_map/reshape | solution.py:125
  (74 shorter events, 55.5 us)
Async XLA Ops:
  0.0 61.6 %copy-start = (bf16[3,3,320,320]{3,2,1,0:T(8,128)(2,1)S(1)}, bf16[3,3,320,320]{3,2,1,0:T(8,128)(2,1)}, u32[]{:S(2)}) copy-start(bf16[3,3,320,320]{3,2,1,0:T(8,128)(2,1)} %param.12) | copy-start | bytes 5529604
  0.0 4.6 %copy-start.14 = (f32[320]{0:T(512)S(1)}, f32[320]{0:T(512)}, u32[]{:S(2)}) copy-start(f32[320]{0:T(512)} %param.11) | copy-start | bytes 3844
  2.7 1.9 copy-start.2
  5.5 1.1 copy-start.3
  9.9 18.2 %collective-permute-start.1 = (bf16[4,1,240,320]{2,3,1,0:T(8,128)(2,1)}, bf16[4,1,240,320]{2,3,1,0:T(8,128)(2,1)}, u32[]{:S(2)}, u32[]{:S(2)}) collective-permute-start(bf16[4,1,240,320]{2,3,1,0:T(8,128)(2,1)} %copy.66), channel_id=1, source_target_pairs={{1,0},{2,1},{3,2},{4,3},{5,4},{6,5},{7,6},{8,7},{9,8},{10,9},{11,1... | collective-permute-start | bytes 1843208 | tf_op jit(solution)/shard_map/ppermute | solution.py:19
  13.0 31.9 %collective-permute-start = (bf16[4,1,240,320]{2,3,1,0:T(8,128)(2,1)}, bf16[4,1,240,320]{2,3,1,0:T(8,128)(2,1)}, u32[]{:S(2)}, u32[]{:S(2)}) collective-permute-start(bf16[4,1,240,320]{2,3,1,0:T(8,128)(2,1)} %copy.65), channel_id=1, source_target_pairs={{0,1},{1,2},{2,3},{3,4},{4,5},{5,6},{6,7},{7,8},{8,9},{9,10},{10,1... | collective-permute-start | bytes 1843208 | tf_op jit(solution)/shard_map/ppermute | solution.py:17
  59.2 2.4 copy-start.16
  77.8 3.4 copy-start.13
  100.9 1.1 copy-start.5
  102.9 15.3 %collective-permute-start.3 = (bf16[1,480,320]{1,2,0:T(8,128)(2,1)}, bf16[1,480,320]{1,2,0:T(8,128)(2,1)S(1)}, u32[]{:S(2)}, u32[]{:S(2)}) collective-permute-start(bf16[1,480,320]{1,2,0:T(8,128)(2,1)} %get-tuple-element.13), channel_id=1, source_target_pairs={{16,0},{32,16},{48,32},{64,48},{80,64},{96,80},{112,96},{128,112},... | collective-permute-start | bytes 921608 | tf_op jit(solution)/shard_map/ppermute | solution.py:19
  106.3 11.9 %collective-permute-start.2 = (bf16[1,480,320]{1,2,0:T(8,128)(2,1)}, bf16[1,480,320]{1,2,0:T(8,128)(2,1)}, u32[]{:S(2)}, u32[]{:S(2)}) collective-permute-start(bf16[1,480,320]{1,2,0:T(8,128)(2,1)} %get-tuple-element.14), channel_id=1, source_target_pairs={{0,16},{16,32},{32,48},{48,64},{64,80},{80,96},{96,112},{112,128},... | collective-permute-start | bytes 921608 | tf_op jit(solution)/shard_map/ppermute | solution.py:17
  114.5 3.7 copy-start.6
  134.0 3.2 copy-start.7
  152.8 2.4 copy-start.15
  155.2 4.3 %copy-start.10 = (bf16[320,320]{1,0:T(8,128)(2,1)S(1)}, bf16[320,320]{1,0:T(8,128)(2,1)}, u32[]{:S(2)}) copy-start(bf16[320,320]{1,0:T(8,128)(2,1)} %param.17) | copy-start | bytes 614404
  164.6 16.9 %copy-start.11 = (bf16[320,320]{1,0:T(8,128)(2,1)S(1)}, bf16[320,320]{1,0:T(8,128)(2,1)}, u32[]{:S(2)}) copy-start(bf16[320,320]{1,0:T(8,128)(2,1)} %param.16) | copy-start | bytes 614404
  166.8 54.5 %all-to-all-start.2 = ((bf16[4,16,30,320]{3,0,2,1:T(4,128)(2,1)}), bf16[4,16,30,320]{3,0,2,1:T(4,128)(2,1)}, u32[]{:S(2)}, u32[]{:S(2)}) async-start(bf16[4,16,30,320]{3,0,2,1:T(4,128)(2,1)} %copy.86), calls=%async_computation.2 | async-start | bytes 2949120 | tf_op jit(solution)/shard_map/all_to_all | solution.py:118
  186.4 39.9 %copy-start.12 = (bf16[320,320]{1,0:T(8,128)(2,1)S(1)}, bf16[320,320]{1,0:T(8,128)(2,1)}, u32[]{:S(2)}) copy-start(bf16[320,320]{1,0:T(8,128)(2,1)} %param.18) | copy-start | bytes 614404
  221.3 42.2 %all-to-all-start.1 = ((bf16[4,16,30,320]{3,0,2,1:T(4,128)(2,1)}), bf16[4,16,30,320]{3,0,2,1:T(4,128)(2,1)S(1)}, u32[]{:S(2)}, u32[]{:S(2)}) async-start(bf16[4,16,30,320]{3,0,2,1:T(4,128)(2,1)} %copy.83), calls=%async_computation.1 | async-start | bytes 2949120 | tf_op jit(solution)/shard_map/all_to_all | solution.py:117
  263.5 42.3 %all-to-all-start = ((bf16[4,16,30,320]{3,0,2,1:T(4,128)(2,1)}), bf16[4,16,30,320]{3,0,2,1:T(4,128)(2,1)S(1)}, u32[]{:S(2)}, u32[]{:S(2)}) async-start(bf16[4,16,30,320]{3,0,2,1:T(4,128)(2,1)} %copy.80), calls=%async_computation | async-start | bytes 2949120 | tf_op jit(solution)/shard_map/all_to_all | solution.py:119
  314.9 2.1 copy-start.8
  368.7 5.6 %copy-start.4 = (f32[1920,320]{0,1:T(8,128)S(1)}, f32[1920,320]{0,1:T(8,128)}, u32[]{:S(2)}) copy-start(f32[1920,320]{0,1:T(8,128)} %get-tuple-element.6) | copy-start | bytes 7372804
  368.7 5.6 %copy-start.9 = (bf16[320,320]{1,0:T(8,128)(2,1)S(1)}, bf16[320,320]{1,0:T(8,128)(2,1)}, u32[]{:S(2)}) copy-start(bf16[320,320]{1,0:T(8,128)(2,1)} %param.19) | copy-start | bytes 614404
  378.0 10.9 %copy-start.1 = (bf16[3,3,320,320]{3,2,1,0:T(8,128)(2,1)S(1)}, bf16[3,3,320,320]{3,2,1,0:T(8,128)(2,1)}, u32[]{:S(2)}) copy-start(bf16[3,3,320,320]{3,2,1,0:T(8,128)(2,1)} %param.12) | copy-start | bytes 5529604
where the time goes:
time: 395 us; the launch traced here: 389 us
  local copies, waits for them, and re-layouts  143 us (36%)
  waiting for transfers between devices  108 us (27%)
  blocking collectives  44.2 us (11%)
  starting transfers between devices  36.9 us (9%)
  matrix products  31.5 us (8%)
  other arithmetic  25 us (6%)
    all_to_all x1, blocking collectives, local(): lax.all_to_all(attended, 'frame', split_axis=0, concat_axis=1, tiled=True)  44.2 us
    all_to_all x1, waiting for transfers between devices, local(): lax.all_to_all(triple[1], 'frame', split_axis=1, concat_axis=0, tiled=True)  32.6 us
    all_to_all x1, waiting for transfers between devices, local(): lax.all_to_all(triple[0], 'frame', split_axis=1, concat_axis=0, tiled=True)  27.8 us
    all_to_all x1, waiting for transfers between devices, local(): lax.all_to_all(triple[2], 'frame', split_axis=1, concat_axis=0, tiled=True)  20.7 us
    ppermute x2, waiting for transfers between devices, extended(): lax.ppermute(tail, axis, [(i, (i + 1) % count) for i in range(ends)])  15.3 us
    all_to_all x1, starting transfers between devices, local(): lax.all_to_all(triple[1], 'frame', split_axis=1, concat_axis=0, tiled=True)  14.6 us
    reshape x2, local copies, waits for them, and re-layouts, temporal_mix(): return total.reshape(frames, pixels, chans)  12.4 us
    ppermute x2, waiting for transfers between devices, extended(): lax.ppermute(head, axis, [((i + 1) % count, i) for i in range(ends)])  11.6 us
  transfers between devices with their start and end apart: 7, of which 5 were waited for; matrix products, arithmetic and copies ran while one was open for 11% of the time, Pallas kernels for 0%

commit v1 on v0

--- a/solution.py
+++ b/solution.py
@@ -4,6 +4,13 @@
 from jax.sharding import PartitionSpec as P
 
 HEAD_DIM = 64
+
+
+def exchange_blocks(x, mesh_axis, split, join):
+    count = lax.axis_size(mesh_axis)
+    blocks = jnp.stack(jnp.split(x, count, axis=split), axis=0)
+    blocks = lax.all_to_all(blocks, mesh_axis, split_axis=0, concat_axis=0)
+    return jnp.concatenate(blocks, axis=join)
 
 
 def extended(cells, sides, width):
@@ -115,7 +122,7 @@
     attended = attend_triple(
         (
             lax.all_to_all(triple[0], "frame", split_axis=1, concat_axis=0, tiled=True),
-            lax.all_to_all(triple[1], "frame", split_axis=1, concat_axis=0, tiled=True),
+            exchange_blocks(triple[1], "frame", 1, 0),
             lax.all_to_all(triple[2], "frame", split_axis=1, concat_axis=0, tiled=True),
         )
     )

time: 395 us -> 395 us (level)
  no operation moved by 1% of the time
where the time goes in v1:
time: 395 us; the launch traced here: 389 us
  local copies, waits for them, and re-layouts  143 us (36%)
  waiting for transfers between devices  108 us (27%)
  blocking collectives  44.2 us (11%)
  starting transfers between devices  36.9 us (9%)
  matrix products  31.6 us (8%)
  other arithmetic  25 us (6%)
    all_to_all x1, blocking collectives, local(): lax.all_to_all(attended, 'frame', split_axis=0, concat_axis=1, tiled=True)  44.2 us
    all_to_all x1, waiting for transfers between devices, exchange_blocks(): blocks = lax.all_to_all(blocks, mesh_axis, split_axis=0, concat_axis=0)  32.6 us
    all_to_all x1, waiting for transfers between devices, local(): lax.all_to_all(triple[0], 'frame', split_axis=1, concat_axis=0, tiled=True)  27.8 us
    all_to_all x1, waiting for transfers between devices, local(): lax.all_to_all(triple[2], 'frame', split_axis=1, concat_axis=0, tiled=True)  20.7 us
    ppermute x2, waiting for transfers between devices, extended(): lax.ppermute(tail, axis, [(i, (i + 1) % count) for i in range(ends)])  15.3 us
    all_to_all x1, starting transfers between devices, exchange_blocks(): blocks = lax.all_to_all(blocks, mesh_axis, split_axis=0, concat_axis=0)  14.6 us
    reshape x2, local copies, waits for them, and re-layouts, temporal_mix(): return total.reshape(frames, pixels, chans)  12.4 us
    ppermute x2, waiting for transfers between devices, extended(): lax.ppermute(head, axis, [((i + 1) % count, i) for i in range(ends)])  11.6 us
  transfers between devices with their start and end apart: 7, of which 5 were waited for; matrix products, arithmetic and copies ran while one was open for 11% of the time, Pallas kernels for 0%

profile of v1, /device:TPU:39, one launch (start us, length us, event | category | flops | bytes accessed | tf_op | source)
XLA Modules:
  0.0 389.2 jit_solution(7045659449236924321)
XLA Ops:
  0.0 2.7 copy.111
  13.0 3.5 collective-permute-start
  16.5 11.6 %collective-permute-done.1 = bf16[4,1,240,320]{2,3,1,0:T(8,128)(2,1)} collective-permute-done((bf16[4,1,240,320]{2,3,1,0:T(8,128)(2,1)}, bf16[4,1,240,320]{2,3,1,0:T(8,128)(2,1)}, u32[]{:S(2)}, u32[]{:S(2)}) %collective-permute-start.1) | collective-permute-done | bytes 614432 | tf_op jit(solution)/shard_map/ppermute | solution.py:26
  29.5 15.3 %collective-permute-done = bf16[4,1,240,320]{2,3,1,0:T(8,128)(2,1)} collective-permute-done((bf16[4,1,240,320]{2,3,1,0:T(8,128)(2,1)}, bf16[4,1,240,320]{2,3,1,0:T(8,128)(2,1)}, u32[]{:S(2)}, u32[]{:S(2)}) %collective-permute-start) | collective-permute-done | bytes 614432 | tf_op jit(solution)/shard_map/ppermute | solution.py:24
  49.2 2.9 pad
  52.1 5.8 %reshape.115 = bf16[4,4,8,31,320]{4,3,2,1,0:T(8,128)(2,1)} reshape(bf16[4,4,248,320]{3,2,1,0:T(8,128)(2,1)} %pad) | data formatting | bytes 5079040 | tf_op jit(solution)/shard_map/conv_general_dilated | solution.py:91
  61.6 6.6 %fusion.24 = f32[2,32,31,320]{3,1,2,0:T(8,128)S(1)} fusion(bf16[3,3,320,320]{3,2,1,0:T(8,128)(2,1)S(1)} %copy-done, bf16[4,4,8,33,320]{4,3,2,1,0:T(8,128)(2,1)S(1)} %fusion.4, pred[32,31]{0,1:T(8,128)(4,1)S(1)} %copy-done.16), kind=kOutput, calls=%fused_computation.43 | convolution fusion | flops 3657543680 | bytes 7087072 | tf_op jit(solution)/shard_map/conv_general_dilated | solution.py:91
  71.7 2.8 multiply_reduce_fusion.2
  74.5 3.3 copy.119
  77.8 3.4 copy.118
  83.1 4.9 %copy.122 = bf16[4,2,240,320]{2,1,0,3:T(2,128)(2,1)} copy(bf16[4,2,240,320]{3,2,0,1:T(8,128)(2,1)} %multiply_convert_fusion) | data formatting | bytes 2457600 | tf_op jit(solution)/shard_map/convert_element_type | solution.py:102
  88.0 5.3 %convert_element_type.48 = bf16[1920,320]{0,1:T(8,128)(2,1)} reshape(bf16[4,2,240,320]{2,1,0,3:T(2,128)(2,1)} %copy.122) | data formatting | bytes 2457600 | tf_op jit(solution)/shard_map/convert_element_type | solution.py:102
  93.3 4.8 %reshape.107 = f32[4,480,320]{1,2,0:T(8,128)} reshape(f32[4,2,240,320]{2,1,3,0:T(2,128)} %copy.119) | data formatting | bytes 4915200 | tf_op jit(solution)/shard_map/reshape | solution.py:101
  98.2 2.6 multiply_convert_fusion.1
  102.9 3.4 collective-permute-start.3
  106.3 3.1 collective-permute-start.2
  109.4 5.1 %reshape.106 = f32[1920,320]{0,1:T(8,128)} reshape(f32[4,2,240,320]{2,1,0,3:T(2,128)} %copy.118) | data formatting | bytes 4915200 | tf_op jit(solution)/shard_map/reshape | solution.py:101
  114.5 3.7 fusion.32
  122.6 3.9 %reshape.108 = bf16[1920,320]{0,1:T(8,128)(2,1)} reshape(bf16[4,480,320]{1,0,2:T(4,128)(2,1)} %copy.121) | data formatting | bytes 2457600 | tf_op jit(solution)/shard_map/reshape | solution.py:68
  126.6 3.4 copy.123
  130.0 4.0 %reshape.109 = bf16[1920,320]{0,1:T(8,128)(2,1)} reshape(bf16[4,480,320]{1,0,2:T(4,128)(2,1)} %copy.123) | data formatting | bytes 2457600 | tf_op jit(solution)/shard_map/reshape | solution.py:68
  134.0 3.2 convolution_add_fusion.2
  137.2 3.3 convolution_add_fusion.1
  140.4 6.7 %reshape.110 = f32[4,2,240,320]{2,1,0,3:T(2,128)} reshape(f32[1920,320]{0,1:T(8,128)} %convolution_add_fusion.1) | data formatting | bytes 4915200 | tf_op jit(solution)/shard_map/reshape | solution.py:72
  147.1 5.7 %copy.124 = f32[4,2,240,320]{3,2,0,1:T(8,128)} copy(f32[4,2,240,320]{2,1,0,3:T(2,128)} %reshape.110) | data formatting | bytes 4915200 | tf_op jit(solution)/shard_map/reshape | solution.py:72
  155.3 4.3 %multiply_convert_fusion.2 = (bf16[1920,320]{0,1:T(8,128)(2,1)S(1)}, f32[1920,320]{0,1:T(8,128)}) fusion(f32[320]{0:T(512)S(1)} %copy-done.15, f32[1920]{0:T(1024)S(1)} %rsqrt.35, f32[1920,320]{0,1:T(8,128)} %reshape.106, f32[1920,320]{0,1:T(8,128)} %convolution_add_fusion.1), kind=kLoop, calls=%fused_computation.42 | loop fusion | flops 2457600 | bytes 8610560 | tf_op jit(solution)/shard_map/convert_element_type | solution.py:106
  162.0 2.5 reshape_reshape.19
  166.9 14.6 %all-to-all-start.2 = ((bf16[16,4,1,30,320]{4,1,3,2,0:T(4,128)(2,1)}), bf16[16,4,1,30,320]{4,1,3,2,0:T(4,128)(2,1)}, u32[]{:S(2)}, u32[]{:S(2)}) async-start(bf16[16,4,1,30,320]{4,1,3,2,0:T(4,128)(2,1)} %copy.149), calls=%async_computation.2 | async-start | bytes 2949120 | tf_op jit(solution)/shard_map/all_to_all | solution.py:12
  183.9 2.5 reshape_reshape.17
  188.7 32.6 %all-to-all-done.2 = bf16[16,4,1,30,320]{4,1,3,2,0:T(4,128)(2,1)} async-done(((bf16[16,4,1,30,320]{4,1,3,2,0:T(4,128)(2,1)}), bf16[16,4,1,30,320]{4,1,3,2,0:T(4,128)(2,1)}, u32[]{:S(2)}, u32[]{:S(2)}) %all-to-all-start.2) | async-done | bytes 1228832 | tf_op jit(solution)/shard_map/all_to_all | solution.py:12
  221.4 5.0 %all-to-all-start.1 = ((bf16[4,16,30,320]{3,0,2,1:T(4,128)(2,1)}), bf16[4,16,30,320]{3,0,2,1:T(4,128)(2,1)S(1)}, u32[]{:S(2)}, u32[]{:S(2)}) async-start(bf16[4,16,30,320]{3,0,2,1:T(4,128)(2,1)} %copy.130), calls=%async_computation.1 | async-start | bytes 2949120 | tf_op jit(solution)/shard_map/all_to_all | solution.py:124
  228.3 2.5 copy.126
  230.8 2.5 reshape_reshape.15
  235.7 27.8 %all-to-all-done.1 = bf16[4,16,30,320]{3,0,2,1:T(4,128)(2,1)S(1)} async-done(((bf16[4,16,30,320]{3,0,2,1:T(4,128)(2,1)}), bf16[4,16,30,320]{3,0,2,1:T(4,128)(2,1)S(1)}, u32[]{:S(2)}, u32[]{:S(2)}) %all-to-all-start.1) | async-done | bytes 1228832 | tf_op jit(solution)/shard_map/all_to_all | solution.py:124
  263.5 5.3 %all-to-all-start = ((bf16[4,16,30,320]{3,0,2,1:T(4,128)(2,1)}), bf16[4,16,30,320]{3,0,2,1:T(4,128)(2,1)S(1)}, u32[]{:S(2)}, u32[]{:S(2)}) async-start(bf16[4,16,30,320]{3,0,2,1:T(4,128)(2,1)} %copy.127), calls=%async_computation | async-start | bytes 2949120 | tf_op jit(solution)/shard_map/all_to_all | solution.py:126
  268.8 3.3 copy.150
  272.1 5.5 %reshape_reshape_reshape.3 = bf16[64,30,5,64]{3,2,0,1:T(8,128)(2,1)} reshape(bf16[16,4,1,30,320]{4,1,0,3,2:T(4,128)(2,1)} %copy.150) | data formatting | bytes 2457600 | tf_op jit(solution)/shard_map/reshape;reshape;reshape | solution.py:48
  279.6 5.5 %reshape_reshape.18 = bf16[64,30,5,64]{3,2,0,1:T(8,128)(2,1)} reshape(bf16[16,4,1,30,320]{4,1,0,3,2:T(4,128)(2,1)} %copy.131) | data formatting | bytes 2457600 | tf_op jit(solution)/shard_map/reshape;reshape | solution.py:47
  285.1 20.7 %all-to-all-done = bf16[4,16,30,320]{3,0,2,1:T(4,128)(2,1)S(1)} async-done(((bf16[4,16,30,320]{3,0,2,1:T(4,128)(2,1)}), bf16[4,16,30,320]{3,0,2,1:T(4,128)(2,1)S(1)}, u32[]{:S(2)}, u32[]{:S(2)}) %all-to-all-start) | async-done | bytes 1228832 | tf_op jit(solution)/shard_map/all_to_all | solution.py:126
  306.6 3.6 reshape_reshape.16
  310.2 4.7 %multiply_reduce_fusion = (f32[30,5,64]{2,1,0:T(8,128)S(1)}, f32[30,5,64,64]{2,3,1,0:T(8,128)S(1)}) fusion(bf16[64,30,5,64]{3,2,0,1:T(8,128)(2,1)} %reshape_reshape_reshape.3, bf16[64,30,5,64]{3,2,0,1:T(8,128)(2,1)} %reshape_reshape.18), kind=kOutput, calls=%fused_computation.5 | convolution fusion | flops 79862400 | bytes 4953600 | tf_op jit(solution)/shard_map/fphd,gphd->phfg/dot_general | solution.py:50
  317.1 2.7 fusion.1
  319.8 3.9 %copy.155 = bf16[64,1,30,320]{3,2,1,0:T(8,128)(2,1)S(1)} copy(bf16[64,1,30,320]{0,3,2,1:T(8,128)(2,1)} %bitcast.169) | data formatting | bytes 2457600 | tf_op jit(solution)/shard_map/convert_element_type | solution.py:59
  323.7 44.2 %all_to_all.50 = bf16[64,1,30,320]{3,2,1,0:T(8,128)(2,1)S(1)} all-to-all(bf16[64,1,30,320]{3,2,1,0:T(8,128)(2,1)S(1)} %copy.155), channel_id=1, replica_groups=mesh['frame'=16,'row'=16] {'frame'}, dimensions={0} | all-to-all | bytes 2457600 | tf_op jit(solution)/shard_map/all_to_all | solution.py:129
  370.8 3.5 reshape.111
  374.3 3.7 convolution_add_fusion
  378.0 6.9 %reshape.112 = f32[4,2,240,320]{2,1,0,3:T(2,128)} reshape(f32[1920,320]{0,1:T(8,128)} %convolution_add_fusion) | data formatting | bytes 4915200 | tf_op jit(solution)/shard_map/reshape | solution.py:132
  384.9 4.1 %copy.158 = f32[4,2,240,320]{2,3,1,0:T(8,128)} copy(f32[4,2,240,320]{2,1,0,3:T(2,128)} %reshape.112) | data formatting | bytes 4915200 | tf_op jit(solution)/shard_map/reshape | solution.py:132
  (90 shorter events, 55.4 us)
Async XLA Ops:
  0.0 61.6 %copy-start = (bf16[3,3,320,320]{3,2,1,0:T(8,128)(2,1)S(1)}, bf16[3,3,320,320]{3,2,1,0:T(8,128)(2,1)}, u32[]{:S(2)}) copy-start(bf16[3,3,320,320]{3,2,1,0:T(8,128)(2,1)} %param.12) | copy-start | bytes 5529604
  0.0 4.6 %copy-start.14 = (f32[320]{0:T(512)S(1)}, f32[320]{0:T(512)}, u32[]{:S(2)}) copy-start(f32[320]{0:T(512)} %param.11) | copy-start | bytes 3844
  2.7 1.9 copy-start.2
  5.5 1.1 copy-start.3
  9.9 18.2 %collective-permute-start.1 = (bf16[4,1,240,320]{2,3,1,0:T(8,128)(2,1)}, bf16[4,1,240,320]{2,3,1,0:T(8,128)(2,1)}, u32[]{:S(2)}, u32[]{:S(2)}) collective-permute-start(bf16[4,1,240,320]{2,3,1,0:T(8,128)(2,1)} %copy.113), channel_id=1, source_target_pairs={{1,0},{2,1},{3,2},{4,3},{5,4},{6,5},{7,6},{8,7},{9,8},{10,9},{11,1... | collective-permute-start | bytes 1843208 | tf_op jit(solution)/shard_map/ppermute | solution.py:26
  13.0 31.9 %collective-permute-start = (bf16[4,1,240,320]{2,3,1,0:T(8,128)(2,1)}, bf16[4,1,240,320]{2,3,1,0:T(8,128)(2,1)}, u32[]{:S(2)}, u32[]{:S(2)}) collective-permute-start(bf16[4,1,240,320]{2,3,1,0:T(8,128)(2,1)} %copy.112), channel_id=1, source_target_pairs={{0,1},{1,2},{2,3},{3,4},{4,5},{5,6},{6,7},{7,8},{8,9},{9,10},{10,1... | collective-permute-start | bytes 1843208 | tf_op jit(solution)/shard_map/ppermute | solution.py:24
  59.2 2.4 copy-start.16
  77.8 3.4 copy-start.13
  100.9 1.1 copy-start.5
  102.9 15.3 %collective-permute-start.3 = (bf16[1,480,320]{1,2,0:T(8,128)(2,1)}, bf16[1,480,320]{1,2,0:T(8,128)(2,1)S(1)}, u32[]{:S(2)}, u32[]{:S(2)}) collective-permute-start(bf16[1,480,320]{1,2,0:T(8,128)(2,1)} %get-tuple-element.13), channel_id=1, source_target_pairs={{16,0},{32,16},{48,32},{64,48},{80,64},{96,80},{112,96},{128,112},... | collective-permute-start | bytes 921608 | tf_op jit(solution)/shard_map/ppermute | solution.py:26
  106.3 11.9 %collective-permute-start.2 = (bf16[1,480,320]{1,2,0:T(8,128)(2,1)}, bf16[1,480,320]{1,2,0:T(8,128)(2,1)}, u32[]{:S(2)}, u32[]{:S(2)}) collective-permute-start(bf16[1,480,320]{1,2,0:T(8,128)(2,1)} %get-tuple-element.14), channel_id=1, source_target_pairs={{0,16},{16,32},{32,48},{48,64},{64,80},{80,96},{96,112},{112,128},... | collective-permute-start | bytes 921608 | tf_op jit(solution)/shard_map/ppermute | solution.py:24
  114.5 3.7 copy-start.6
  134.0 3.2 copy-start.7
  152.8 2.4 copy-start.15
  155.2 4.3 %copy-start.10 = (bf16[320,320]{1,0:T(8,128)(2,1)S(1)}, bf16[320,320]{1,0:T(8,128)(2,1)}, u32[]{:S(2)}) copy-start(bf16[320,320]{1,0:T(8,128)(2,1)} %param.17) | copy-start | bytes 614404
  165.0 16.5 %copy-start.11 = (bf16[320,320]{1,0:T(8,128)(2,1)S(1)}, bf16[320,320]{1,0:T(8,128)(2,1)}, u32[]{:S(2)}) copy-start(bf16[320,320]{1,0:T(8,128)(2,1)} %param.16) | copy-start | bytes 614404
  166.9 54.5 %all-to-all-start.2 = ((bf16[16,4,1,30,320]{4,1,3,2,0:T(4,128)(2,1)}), bf16[16,4,1,30,320]{4,1,3,2,0:T(4,128)(2,1)}, u32[]{:S(2)}, u32[]{:S(2)}) async-start(bf16[16,4,1,30,320]{4,1,3,2,0:T(4,128)(2,1)} %copy.149), calls=%async_computation.2 | async-start | bytes 2949120 | tf_op jit(solution)/shard_map/all_to_all | solution.py:12
  186.5 39.9 %copy-start.12 = (bf16[320,320]{1,0:T(8,128)(2,1)S(1)}, bf16[320,320]{1,0:T(8,128)(2,1)}, u32[]{:S(2)}) copy-start(bf16[320,320]{1,0:T(8,128)(2,1)} %param.18) | copy-start | bytes 614404
  221.4 42.2 %all-to-all-start.1 = ((bf16[4,16,30,320]{3,0,2,1:T(4,128)(2,1)}), bf16[4,16,30,320]{3,0,2,1:T(4,128)(2,1)S(1)}, u32[]{:S(2)}, u32[]{:S(2)}) async-start(bf16[4,16,30,320]{3,0,2,1:T(4,128)(2,1)} %copy.130), calls=%async_computation.1 | async-start | bytes 2949120 | tf_op jit(solution)/shard_map/all_to_all | solution.py:124
  263.5 42.3 %all-to-all-start = ((bf16[4,16,30,320]{3,0,2,1:T(4,128)(2,1)}), bf16[4,16,30,320]{3,0,2,1:T(4,128)(2,1)S(1)}, u32[]{:S(2)}, u32[]{:S(2)}) async-start(bf16[4,16,30,320]{3,0,2,1:T(4,128)(2,1)} %copy.127), calls=%async_computation | async-start | bytes 2949120 | tf_op jit(solution)/shard_map/all_to_all | solution.py:126
  315.0 2.1 copy-start.8
  368.7 5.6 %copy-start.4 = (f32[1920,320]{0,1:T(8,128)S(1)}, f32[1920,320]{0,1:T(8,128)}, u32[]{:S(2)}) copy-start(f32[1920,320]{0,1:T(8,128)} %get-tuple-element.6) | copy-start | bytes 7372804
  368.7 5.6 %copy-start.9 = (bf16[320,320]{1,0:T(8,128)(2,1)S(1)}, bf16[320,320]{1,0:T(8,128)(2,1)}, u32[]{:S(2)}) copy-start(bf16[320,320]{1,0:T(8,128)(2,1)} %param.19) | copy-start | bytes 614404
  378.0 10.9 %copy-start.1 = (bf16[3,3,320,320]{3,2,1,0:T(8,128)(2,1)S(1)}, bf16[3,3,320,320]{3,2,1,0:T(8,128)(2,1)}, u32[]{:S(2)}) copy-start(bf16[3,3,320,320]{3,2,1,0:T(8,128)(2,1)} %param.12) | copy-start | bytes 5529604
